TPU v7x, 128 devices: a whole 4x4x4 slice. The times are simulated.
128 devices in a mesh: leaf: 4 (over y), rows: 32 (over z, x, core).
Axes of the slice: x: 4, y: 4, z: 4, core: 2. Of those that a mesh axis runs over, the one named last changes fastest.
Arguments:
- leaf_rhs: float32 [8, 16, 2048], P(None, 'leaf', 'rows'), may hold values from -6 to 6
- parent_rhs: float32 [8, 4, 4096], P(None, 'leaf', 'rows'), may hold values from -6 to 6
- root_rhs: float32 [8, 4096], P(None, ('leaf', 'rows')), may hold values from -6 to 6
- leaf_inv: bfloat16 [16, 2048, 2048], P('leaf', 'rows'), as said below
- leaf_panel: bfloat16 [16, 8192, 2048], P('leaf', 'rows'), may hold values from -0.0625 to 0.0625
- leaf_rows: int32 [16, 8192], P('leaf', 'rows'), may hold values from 0 to 8191, as said below
- leaf_height: int32 [16], P('leaf'), may hold values from 2048 to 8192
- parent_inv: bfloat16 [4, 4096, 4096], P('leaf', 'rows'), as said below
- parent_panel: bfloat16 [4, 4096, 4096], P('leaf', 'rows'), may hold values from -0.046875 to 0.046875
- parent_rows: int32 [4, 4096], P('leaf', 'rows'), may hold values from 0 to 4095, as said below
- parent_height: int32 [4], P('leaf'), may hold values from 1024 to 4096
- root_inv: bfloat16 [4096, 4096], P('rows'), as said below
Outputs:
- leaf_solution: float32 [8, 16, 2048], P(None, 'leaf', 'rows')
- parent_solution: float32 [8, 4, 4096], P(None, 'leaf', 'rows')
- root_solution: float32 [8, 4096], P(None, ('leaf', 'rows'))
Inputs may be any that keep to these rules, and one draw needn't show every extreme that they name: `leaf_rows`: each leaf's first leaf_height entries are distinct and ascending; every entry is a valid ancestor index. `parent_rows`: each parent's first parent_height entries are distinct and ascending. `leaf_inv`: A dense well conditioned matrix. `parent_inv`: A dense well conditioned matrix. `root_inv`: A dense well conditioned matrix.
All inputs are finite; a program needn't handle non-finite values.
Results may differ from a plain program's by a relative error of at most 0.009.
Values may be sent and summed in bfloat16 or wider, within the bound.
A program may use at most 64 MiB of HBM per device.

v0:
```python
import jax
import jax.numpy as jnp
from jax import lax
from jax.sharding import PartitionSpec as P


def shards(
    leaf_rhs,
    parent_rhs,
    root_rhs,
    leaf_inv,
    leaf_panel,
    leaf_rows,
    leaf_height,
    parent_inv,
    parent_panel,
    parent_rows,
    parent_height,
    root_inv,
):
    rcount = leaf_rhs.shape[0]
    group_leaves = leaf_rhs.shape[1]
    leaf_local = leaf_panel.shape[1]
    parent_width = parent_inv.shape[2]
    root_width = root_inv.shape[1]
    row_index = lax.axis_index("rows")
    parent_cols = parent_rhs.shape[2]
    root_cols = root_rhs.shape[1]
    flat_index = lax.axis_index("leaf") * lax.axis_size("rows") + row_index
    block = leaf_inv
    ly = jnp.einsum(
        "rln,lin->rli",
        lax.all_gather(leaf_rhs.astype(jnp.bfloat16), "rows", axis=2, tiled=True),
        block,
        preferred_element_type=jnp.float32,
    )
    lyb = ly.astype(jnp.bfloat16)
    block = leaf_panel
    lupd = jnp.einsum(
        "rln,lhn->rlh",
        lax.all_gather(lyb, "rows", axis=2, tiled=True),
        block,
        preferred_element_type=jnp.float32,
    )
    leaf_pos = row_index * leaf_local + jnp.arange(leaf_local, dtype=jnp.int32)
    leaf_mask = leaf_pos[None, :] < leaf_height[:, None]
    lupd = jnp.where(leaf_mask[None, :, :], lupd, 0.0)
    leaf_flat = leaf_rows.reshape(-1)
    local_acc = (
        jnp.zeros((rcount, parent_width + root_width), jnp.float32)
        .at[:, leaf_flat]
        .add(lupd.reshape(rcount, -1))
    )
    group_acc = lax.psum(local_acc, "rows")
    parent_acc = group_acc[:, :parent_width]
    root_from_leaves = lax.psum(group_acc[:, parent_width:], "leaf")
    parent_slice = lax.dynamic_slice_in_dim(parent_acc, row_index * parent_cols, parent_cols, 1)
    prb = (parent_rhs[:, 0, :] - parent_slice).astype(jnp.bfloat16)
    inverse_rows = parent_inv[0]
    panel_rows = parent_panel[0]
    block = inverse_rows
    py = jnp.dot(
        lax.all_gather(prb, "rows", axis=1, tiled=True), block.T, preferred_element_type=jnp.float32
    )
    pyb = py.astype(jnp.bfloat16)
    parent_local = panel_rows.shape[0]
    block = panel_rows
    pupd = jnp.dot(
        lax.all_gather(pyb, "rows", axis=1, tiled=True), block.T, preferred_element_type=jnp.float32
    )
    parent_pos = row_index * parent_local + jnp.arange(parent_local, dtype=jnp.int32)
    parent_mask = parent_pos < parent_height[0]
    pupd = jnp.where(parent_mask[None, :], pupd, 0.0)
    parent_root = jnp.zeros((rcount, root_width), jnp.float32).at[:, parent_rows[0]].add(pupd)
    root_acc = root_from_leaves + lax.psum(parent_root, ("leaf", "rows"))
    root_slice = lax.dynamic_slice_in_dim(root_acc, flat_index * root_cols, root_cols, 1)
    rrb = (root_rhs - root_slice).astype(jnp.bfloat16)
    block = root_inv
    ry = jnp.dot(
        lax.all_gather(rrb, ("leaf", "rows"), axis=1, tiled=True),
        block.T,
        preferred_element_type=jnp.float32,
    )
    root_term = jnp.dot(ry.astype(jnp.bfloat16), root_inv, preferred_element_type=jnp.float32)
    root_full = lax.psum(root_term, "rows")
    root_solution = lax.dynamic_slice_in_dim(root_full, flat_index * root_cols, root_cols, 1)
    rxb = root_full.astype(jnp.bfloat16)
    parent_anc = rxb[:, parent_rows[0]]
    parent_anc = jnp.where(parent_mask[None, :], parent_anc, jnp.zeros_like(parent_anc))
    parent_term = jnp.dot(parent_anc, panel_rows, preferred_element_type=jnp.float32)
    parent_tail = lax.psum_scatter(parent_term, "rows", scatter_dimension=1, tiled=True)
    pvb = (py - parent_tail).astype(jnp.bfloat16)
    parent_sol_term = jnp.dot(pvb, inverse_rows, preferred_element_type=jnp.float32)
    parent_sol = lax.psum_scatter(parent_sol_term, "rows", scatter_dimension=1, tiled=True)
    parent_whole = lax.all_gather(parent_sol.astype(jnp.bfloat16), "rows", axis=1, tiled=True)
    ancestors = jnp.concatenate([parent_whole, rxb], axis=1)
    leaf_anc = ancestors[:, leaf_flat].reshape(rcount, group_leaves, leaf_local)
    leaf_anc = jnp.where(leaf_mask[None, :, :], leaf_anc, jnp.zeros_like(leaf_anc))
    leaf_term = jnp.einsum("rlh,lhc->rlc", leaf_anc, leaf_panel, preferred_element_type=jnp.float32)
    leaf_tail = lax.psum_scatter(leaf_term, "rows", scatter_dimension=2, tiled=True)
    lvb = (ly - leaf_tail).astype(jnp.bfloat16)
    leaf_sol_term = jnp.einsum("rli,lic->rlc", lvb, leaf_inv, preferred_element_type=jnp.float32)
    leaf_sol = lax.psum_scatter(leaf_sol_term, "rows", scatter_dimension=2, tiled=True)
    return (leaf_sol, parent_sol[:, None, :], root_solution)


def solution(mesh):
    return jax.shard_map(
        shards,
        mesh=mesh,
        in_specs=(
            P(None, "leaf", "rows"),
            P(None, "leaf", "rows"),
            P(None, ("leaf", "rows")),
            P("leaf", "rows", None),
            P("leaf", "rows", None),
            P("leaf", "rows"),
            P("leaf"),
            P("leaf", "rows", None),
            P("leaf", "rows", None),
            P("leaf", "rows"),
            P("leaf"),
            P("rows", None),
        ),
        out_specs=(P(None, "leaf", "rows"), P(None, "leaf", "rows"), P(None, ("leaf", "rows"))),
        check_vma=False,
    )
```

profile of v0, /device:TPU:0, one launch (start us, length us, event | category | flops | bytes accessed | tf_op | source)
XLA Modules:
  0.0 916.0 jit_solution(10626270217796478974)
XLA Ops:
  7.2 0.0 all-reduce.5.cloned.1.call-start
  7.2 0.8 copy.81
  8.0 0.7 copy.91
  8.7 0.1 copy.62
  8.9 27.5 %all_gather.18 = bf16[8,4,2048]{0,1,2:T(4,128)(2,1)S(1)} all-gather(bf16[8,4,64]{0,1,2:T(4,128)(2,1)S(1)} %copy.62), channel_id=1, replica_groups=mesh['leaf'=4,'rows'=32] {'rows'}, dimensions={2}, use_global_device_ids=true | all-gather | bytes 135168 | tf_op jit(solution)/shard_map/all_gather | solution.py:33
  36.4 0.8 fusion.36
  37.1 0.1 copy.64
  37.3 25.3 %all_gather.19 = bf16[8,4,2048]{0,1,2:T(4,128)(2,1)S(1)} all-gather(bf16[8,4,64]{0,1,2:T(4,128)(2,1)S(1)} %copy.64), channel_id=1, replica_groups=mesh['leaf'=4,'rows'=32] {'rows'}, dimensions={2}, use_global_device_ids=true | all-gather | bytes 135168 | tf_op jit(solution)/shard_map/all_gather | solution.py:41
  62.6 0.1 broadcast_compare_fusion
  62.7 3.4 fusion.6
  66.1 0.2 copy.66
  66.3 8.2 scatter_custom_fusion
  74.5 3.5 copy.67
  78.0 0.0 all-reduce.5.cloned.1.call-update
  78.1 0.0 all-reduce.9.cloned.1.call-start
  78.9 100.7 %all-reduce.5.cloned.1.call-done = f32[8,8192]{1,0:T(8,128)} async-done(((f32[8,8192]{1,0:T(8,128)}), f32[8,8192]{1,0:T(8,128)}) %all-reduce.5.cloned.1.call-update) | async-done | bytes 262160 | tf_op jit(solution)/shard_map/psum | solution.py:54
  179.6 1.6 fusion.35
  181.2 24.6 %all_gather.20 = bf16[8,4096]{1,0:T(8,128)(2,1)S(1)} all-gather(bf16[8,128]{1,0:T(8,128)(2,1)S(1)} %subtract_convert_fusion.3), channel_id=1, replica_groups=mesh['leaf'=4,'rows'=32] {'rows'}, dimensions={1}, use_global_device_ids=true | all-gather | bytes 67584 | tf_op jit(solution)/shard_map/all_gather | solution.py:63
  205.9 0.4 fusion.37
  206.2 21.5 %all_gather.21 = bf16[8,4096]{1,0:T(8,128)(2,1)S(1)} all-gather(bf16[8,128]{1,0:T(8,128)(2,1)S(1)} %get-tuple-element.22), channel_id=1, replica_groups=mesh['leaf'=4,'rows'=32] {'rows'}, dimensions={1}, use_global_device_ids=true | all-gather | bytes 67584 | tf_op jit(solution)/shard_map/all_gather | solution.py:69
  227.8 0.4 fusion.12
  228.1 0.1 copy.68
  228.3 1.5 scatter_custom_fusion.1
  229.8 1.2 copy.69
  231.0 0.0 all-reduce.7.cloned.1.call-start
  231.1 0.7 all-reduce.7.cloned.1.call-update
  231.8 0.0 all-reduce.11.cloned.1.call-start
  231.8 141.0 %all-reduce.9.cloned.1.call-done = f32[8,4096]{1,0:T(8,128)} async-done(((f32[8,4096]{1,0:T(8,128)}), f32[8,4096]{1,0:T(8,128)}) %all-reduce.9.cloned.1.call-update) | async-done | bytes 131088 | tf_op jit(solution)/shard_map/psum | solution.py:75
  372.8 41.1 %all-reduce.7.cloned.1.call-done = f32[8,4096]{1,0:T(8,128)} async-done(((f32[8,4096]{1,0:T(8,128)}), f32[8,4096]{1,0:T(8,128)}) %all-reduce.7.cloned.1.call-update) | async-done | bytes 131088 | tf_op jit(solution)/shard_map/psum | solution.py:56
  413.9 0.8 fusion.31
  414.7 35.9 %all-gather = bf16[128,32,8]{1,2,0:T(8,128)(2,1)S(1)} all-gather(bf16[1,32,8]{1,2,0:T(8,128)(2,1)S(1)} %fusion.31), channel_id=1, replica_groups=mesh['leaf'=4,'rows'=32] {'leaf','rows'}, dimensions={0}, use_global_device_ids=true | all-gather | bytes 66048 | tf_op jit(solution)/shard_map/all_gather | solution.py:80
  450.6 0.3 reshape.142
  450.9 3.2 fusion.13
  454.1 0.0 all-reduce.11.cloned.1.call-update
  454.1 0.0 reduce-scatter.9.cloned.1.call-start
  454.2 98.7 %all-reduce.11.cloned.1.call-done = f32[8,4096]{1,0:T(8,128)} async-done(((f32[8,4096]{1,0:T(8,128)}), f32[8,4096]{1,0:T(8,128)}) %all-reduce.11.cloned.1.call-update) | async-done | bytes 131088 | tf_op jit(solution)/shard_map/psum | solution.py:85
  552.9 0.9 convert_element_type.36
  553.8 1.3 copy.71
  555.1 2.0 gather_fusion
  557.1 1.0 fusion.14
  558.1 0.0 reduce-scatter.11.cloned.1.call-start
  558.2 71.9 %reduce-scatter.9.cloned.1.call-done = f32[8,128]{1,0:T(8,128)} async-done(((f32[8,4096]{1,0:T(8,128)}), f32[8,128]{1,0:T(8,128)}) %reduce-scatter.9.cloned.1.call-update) | async-done | bytes 4112 | tf_op jit(solution)/shard_map/reduce_scatter | solution.py:91
  630.1 1.6 fusion.17
  631.7 0.0 reduce-scatter.13.cloned.1.call-start
  631.7 73.8 %reduce-scatter.11.cloned.1.call-done = f32[8,128]{1,0:T(8,128)} async-done(((f32[8,4096]{1,0:T(8,128)}), f32[8,128]{1,0:T(8,128)}) %reduce-scatter.11.cloned.1.call-update) | async-done | bytes 4112 | tf_op jit(solution)/shard_map/reduce_scatter | solution.py:94
  705.5 0.7 convert_element_type.38
  706.2 23.5 %all_gather.23 = bf16[8,4096]{1,0:T(8,128)(2,1)S(1)} all-gather(bf16[8,128]{1,0:T(8,128)(2,1)S(1)} %convert_element_type.38), channel_id=1, replica_groups=mesh['leaf'=4,'rows'=32] {'rows'}, dimensions={1}, use_global_device_ids=true | all-gather | bytes 67584 | tf_op jit(solution)/shard_map/all_gather | solution.py:95
  729.7 1.0 copy.72
  730.7 3.2 gather_fusion.1
  734.0 0.1 copy.73
  734.1 2.8 convolution_bitcast_fusion.1
  736.9 3.1 copy.76
  740.0 4.5 reshape.143
  744.6 0.0 reduce-scatter.15.cloned.1.call-start
  744.6 76.7 %reduce-scatter.13.cloned.1.call-done = f32[64,32]{1,0:T(8,128)} async-done(((f32[2048,32]{1,0:T(8,128)}), f32[64,32]{1,0:T(8,128)}) %reduce-scatter.13.cloned.1.call-update) | async-done | bytes 8208
  821.3 0.9 reshape.144
  822.2 0.1 copy.77
  822.3 0.3 convolution_bitcast_fusion
  822.6 3.1 copy.78
  825.6 4.5 reshape.145
  830.2 1.3 constant_dynamic-slice_fusion
  831.6 76.0 %reduce-scatter.15.cloned.1.call-done = f32[64,32]{1,0:T(8,128)} async-done(((f32[2048,32]{1,0:T(8,128)}), f32[64,32]{1,0:T(8,128)}) %reduce-scatter.15.cloned.1.call-update) | async-done | bytes 8208
  907.6 0.9 reshape.146
  908.5 0.7 copy.74
  (32 shorter events, 0.2 us)
Async XLA Ops:
  7.2 29.2 %copy-start = (bf16[4,64,2048]{2,1,0:T(8,128)(2,1)S(1)}, bf16[4,64,2048]{2,1,0:T(8,128)(2,1)}, u32[]{:S(2)}) copy-start(bf16[4,64,2048]{2,1,0:T(8,128)(2,1)} %param.15) | copy-start | bytes 3145732
  7.2 172.4 %all-reduce.5.cloned.1.call-start = ((), (), s32[]{:S(2)}) async-start(), calls=%async_computation.4 | async-start | bytes 524288 | tf_op jit(solution)/shard_map/psum | solution.py:54
  36.3 26.3 %copy-start.7 = (s32[4]{0:T(128)S(1)}, s32[4]{0:T(128)}, u32[]{:S(2)}) copy-start(s32[4]{0:T(128)} %param.18) | copy-start | bytes 52
  74.5 3.6 copy-start.8
  74.5 106.7 %copy-start.5 = (f32[8,1,128]{2,1,0:T(1,128)S(1)}, f32[8,1,128]{2,1,0:T(1,128)}, u32[]{:S(2)}) copy-start(f32[8,1,128]{2,1,0:T(1,128)} %param.13) | copy-start | bytes 12292
  74.5 131.4 %copy-start.3 = (bf16[1,128,4096]{2,1,0:T(8,128)(2,1)S(1)}, bf16[1,128,4096]{2,1,0:T(8,128)(2,1)}, u32[]{:S(2)}) copy-start(bf16[1,128,4096]{2,1,0:T(8,128)(2,1)} %param.19) | copy-start | bytes 3145732
  78.0 149.7 %copy-start.1 = (bf16[1,128,4096]{2,1,0:T(8,128)(2,1)S(1)}, bf16[1,128,4096]{2,1,0:T(8,128)(2,1)}, u32[]{:S(2)}) copy-start(bf16[1,128,4096]{2,1,0:T(8,128)(2,1)} %param.20) | copy-start | bytes 3145732
  78.1 294.8 %all-reduce.9.cloned.1.call-start = ((), (), s32[]{:S(2)}) async-start(), calls=%async_computation.6 | async-start | bytes 262144 | tf_op jit(solution)/shard_map/psum | solution.py:75
  228.2 185.7 %copy-start.6 = (f32[8,32]{1,0:T(8,128)S(1)}, f32[8,32]{1,0:T(8,128)}, u32[]{:S(2)}) copy-start(f32[8,32]{1,0:T(8,128)} %param.14) | copy-start | bytes 3076
  231.0 182.9 %all-reduce.7.cloned.1.call-start = ((), (), s32[]{:S(2)}) async-start(), calls=%async_computation.5 | async-start | bytes 262144 | tf_op jit(solution)/shard_map/psum | solution.py:56
  231.8 321.1 %all-reduce.11.cloned.1.call-start = ((), (), s32[]{:S(2)}) async-start(), calls=%async_computation.7 | async-start | bytes 262144 | tf_op jit(solution)/shard_map/psum | solution.py:85
  450.6 106.5 %copy-start.2 = (bf16[1,128,4096]{2,1,0:T(8,128)(2,1)S(1)}, bf16[1,128,4096]{2,1,0:T(8,128)(2,1)}, u32[]{:S(2)}) copy-start(bf16[1,128,4096]{2,1,0:T(8,128)(2,1)} %param.20) | copy-start | bytes 3145732
  450.9 179.2 %copy-start.4 = (bf16[1,128,4096]{2,1,0:T(8,128)(2,1)S(1)}, bf16[1,128,4096]{2,1,0:T(8,128)(2,1)}, u32[]{:S(2)}) copy-start(bf16[1,128,4096]{2,1,0:T(8,128)(2,1)} %param.19) | copy-start | bytes 3145732
  454.1 176.0 %reduce-scatter.9.cloned.1.call-start = ((), (), s32[]{:S(2)}) async-start(), calls=%async_computation.8 | async-start | bytes 135168 | tf_op jit(solution)/shard_map/reduce_scatter | solution.py:91
  558.1 147.3 %reduce-scatter.11.cloned.1.call-start = ((), (), s32[]{:S(2)}) async-start(), calls=%async_computation.9 | async-start | bytes 135168 | tf_op jit(solution)/shard_map/reduce_scatter | solution.py:94
  631.7 189.7 %reduce-scatter.13.cloned.1.call-start = ((), (), s32[]{:S(2)}) async-start(), calls=%async_computation.10 | async-start | bytes 1081344
  744.6 163.0 %reduce-scatter.15.cloned.1.call-start = ((), (), s32[]{:S(2)}) async-start(), calls=%async_computation.11 | async-start | bytes 1081344
Sparse Core Ops, SparseCore 0:
  78.2 101.3 all-reduce.4
  231.2 141.6 all-reduce.8
  375.1 38.7 all-reduce.6
  454.2 98.5 all-reduce.10
  558.3 71.7 reduce-scatter.8
  633.9 71.5 reduce-scatter.10
  744.7 76.6 reduce-scatter.12
  830.3 77.2 reduce-scatter.14
where the time goes:
time: 917 us; the launch traced here: 916 us
  waiting for transfers between devices  681 us (74%)
  blocking collectives  158 us (17%)
  local copies, waits for them, and re-layouts  35.6 us (4%)
  between operations  15 us (2%)
  matrix products  13.8 us (2%)
  other arithmetic  12.2 us (1%)
    unnamed x10, waiting for transfers between devices  154 us
    psum x1, waiting for transfers between devices, shards(): root_acc = root_from_leaves + lax.psum(parent_root, ('leaf', 'rows'))  141 us
    psum x1, waiting for transfers between devices, shards(): group_acc = lax.psum(local_acc, 'rows')  101 us
    psum x1, waiting for transfers between devices, shards(): root_full = lax.psum(root_term, 'rows')  98.7 us
    reduce_scatter x1, waiting for transfers between devices, shards(): lax.psum_scatter(parent_sol_term, 'rows', scatter_dimension=1, tiled=True)  73.8 us
    reduce_scatter x1, waiting for transfers between devices, shards(): lax.psum_scatter(parent_term, 'rows', scatter_dimension=1, tiled=True)  71.9 us
    psum x1, waiting for transfers between devices, shards(): root_from_leaves = lax.psum(group_acc[:, parent_width:], 'leaf')  41.1 us
    all_gather x1, blocking collectives, shards(): lax.all_gather(rrb, ('leaf', 'rows'), axis=1, tiled=True)  35.9 us
  transfers between devices with their start and end apart: 8, of which 8 were waited for; matrix products, arithmetic and copies ran while one was open for 0% of the time, Pallas kernels for 0%

commit v1 on v0

--- a/solution.py
+++ b/solution.py
@@ -72,7 +72,7 @@
     parent_mask = parent_pos < parent_height[0]
     pupd = jnp.where(parent_mask[None, :], pupd, 0.0)
     parent_root = jnp.zeros((rcount, root_width), jnp.float32).at[:, parent_rows[0]].add(pupd)
-    root_acc = root_from_leaves + lax.psum(parent_root, ("leaf", "rows"))
+    root_acc = root_from_leaves + lax.psum(lax.psum(parent_root, "rows"), "leaf")
     root_slice = lax.dynamic_slice_in_dim(root_acc, flat_index * root_cols, root_cols, 1)
     rrb = (root_rhs - root_slice).astype(jnp.bfloat16)
     block = root_inv

time: 917 us -> 877 us (0.956)
  waiting for transfers between devices: 681 us -> 640 us
    psum x1, waiting for transfers between devices: 141 us -> 101 us  [shards(): lax.psum(parent_root, 'rows')]
    unnamed x29 -> x31, local copies, waits for them, and re-layouts: 19.6 us -> 19.6 us
where the time goes in v1:
time: 877 us; the launch traced here: 876 us
  waiting for transfers between devices  640 us (73%)
  blocking collectives  158 us (18%)
  local copies, waits for them, and re-layouts  35 us (4%)
  between operations  15 us (2%)
  other arithmetic  13.8 us (2%)
  matrix products  13.8 us (2%)
    unnamed x10, waiting for transfers between devices  153 us
    psum x1, waiting for transfers between devices, shards(): group_acc = lax.psum(local_acc, 'rows')  101 us
    psum x1, waiting for transfers between devices, shards(): lax.psum(parent_root, 'rows')  101 us
    psum x1, waiting for transfers between devices, shards(): root_full = lax.psum(root_term, 'rows')  98.7 us
    reduce_scatter x1, waiting for transfers between devices, shards(): lax.psum_scatter(parent_sol_term, 'rows', scatter_dimension=1, tiled=True)  73.8 us
    reduce_scatter x1, waiting for transfers between devices, shards(): lax.psum_scatter(parent_term, 'rows', scatter_dimension=1, tiled=True)  71.9 us
    psum x1, waiting for transfers between devices, shards(): root_from_leaves = lax.psum(group_acc[:, parent_width:], 'leaf')  41.6 us
    all_gather x1, blocking collectives, shards(): lax.all_gather(rrb, ('leaf', 'rows'), axis=1, tiled=True)  35.9 us
  transfers between devices with their start and end apart: 8, of which 8 were waited for; matrix products, arithmetic and copies ran while one was open for 0% of the time, Pallas kernels for 0%

profile of v1, /device:TPU:0, one launch (start us, length us, event | category | flops | bytes accessed | tf_op | source)
XLA Modules:
  0.0 876.5 jit_solution(8392955872836117848)
XLA Ops:
  7.2 0.0 all-reduce.5.cloned.1.call-start
  7.2 0.8 copy.81
  8.0 0.7 copy.91
  8.7 0.1 copy.62
  8.9 27.5 %all_gather.18 = bf16[8,4,2048]{0,1,2:T(4,128)(2,1)S(1)} all-gather(bf16[8,4,64]{0,1,2:T(4,128)(2,1)S(1)} %copy.62), channel_id=1, replica_groups=mesh['leaf'=4,'rows'=32] {'rows'}, dimensions={2}, use_global_device_ids=true | all-gather | bytes 135168 | tf_op jit(solution)/shard_map/all_gather | solution.py:33
  36.4 0.8 fusion.33
  37.1 0.1 copy.64
  37.3 25.3 %all_gather.19 = bf16[8,4,2048]{0,1,2:T(4,128)(2,1)S(1)} all-gather(bf16[8,4,64]{0,1,2:T(4,128)(2,1)S(1)} %copy.64), channel_id=1, replica_groups=mesh['leaf'=4,'rows'=32] {'rows'}, dimensions={2}, use_global_device_ids=true | all-gather | bytes 135168 | tf_op jit(solution)/shard_map/all_gather | solution.py:41
  62.6 0.1 broadcast_compare_fusion
  62.7 3.4 fusion.6
  66.1 0.2 copy.66
  66.3 8.2 scatter_custom_fusion
  74.5 3.6 copy.67
  78.1 0.0 all-reduce.5.cloned.1.call-update
  78.1 0.0 all-reduce.7.cloned.1.call-start
  78.9 100.8 %all-reduce.5.cloned.1.call-done = f32[8,8192]{1,0:T(8,128)} async-done(((f32[8,8192]{1,0:T(8,128)}), f32[8,8192]{1,0:T(8,128)}) %all-reduce.5.cloned.1.call-update) | async-done | bytes 262160 | tf_op jit(solution)/shard_map/psum | solution.py:54
  179.6 0.9 slice.12
  180.6 24.6 %all_gather.20 = bf16[8,4096]{1,0:T(8,128)(2,1)S(1)} all-gather(bf16[8,128]{1,0:T(8,128)(2,1)S(1)} %subtract_convert_fusion.4), channel_id=1, replica_groups=mesh['leaf'=4,'rows'=32] {'rows'}, dimensions={1}, use_global_device_ids=true | all-gather | bytes 67584 | tf_op jit(solution)/shard_map/all_gather | solution.py:63
  205.2 0.4 fusion.34
  205.6 21.5 %all_gather.21 = bf16[8,4096]{1,0:T(8,128)(2,1)S(1)} all-gather(bf16[8,128]{1,0:T(8,128)(2,1)S(1)} %get-tuple-element.20), channel_id=1, replica_groups=mesh['leaf'=4,'rows'=32] {'rows'}, dimensions={1}, use_global_device_ids=true | all-gather | bytes 67584 | tf_op jit(solution)/shard_map/all_gather | solution.py:69
  227.1 0.4 fusion.12
  227.5 0.1 copy.68
  227.7 1.5 scatter_custom_fusion.1
  229.2 1.2 copy.69
  230.4 0.0 all-reduce.7.cloned.1.call-update
  230.4 0.0 all-reduce.11.cloned.1.call-start
  230.5 100.7 %all-reduce.7.cloned.1.call-done = f32[8,4096]{1,0:T(8,128)} async-done(((f32[8,4096]{1,0:T(8,128)}), f32[8,4096]{1,0:T(8,128)}) %all-reduce.7.cloned.1.call-update) | async-done | bytes 131088 | tf_op jit(solution)/shard_map/psum | solution.py:75
  331.2 1.6 slice_add_fusion
  332.8 0.0 all-reduce.9.cloned.1.call-start
  332.8 41.6 %all-reduce.11.cloned.1.call-done = f32[8,4096]{1,0:T(8,128)} async-done(((f32[8,4096]{1,0:T(8,128)}), f32[8,4096]{1,0:T(8,128)}) %all-reduce.11.cloned.1.call-update) | async-done | bytes 131088 | tf_op jit(solution)/shard_map/psum | solution.py:56
  374.4 0.8 fusion.29
  375.2 35.9 %all-gather = bf16[128,32,8]{1,2,0:T(8,128)(2,1)S(1)} all-gather(bf16[1,32,8]{1,2,0:T(8,128)(2,1)S(1)} %fusion.29), channel_id=1, replica_groups=mesh['leaf'=4,'rows'=32] {'leaf','rows'}, dimensions={0}, use_global_device_ids=true | all-gather | bytes 66048 | tf_op jit(solution)/shard_map/all_gather | solution.py:80
  411.1 0.3 reshape.142
  411.4 3.2 fusion.13
  414.6 0.0 reduce-scatter.9.cloned.1.call-start
  414.6 98.7 %all-reduce.9.cloned.1.call-done = f32[8,4096]{1,0:T(8,128)} async-done(((f32[8,4096]{1,0:T(8,128)}), f32[8,4096]{1,0:T(8,128)}) %all-reduce.9.cloned.1.call-update) | async-done | bytes 131088 | tf_op jit(solution)/shard_map/psum | solution.py:85
  513.3 0.9 convert_element_type.36
  514.2 1.3 copy.71
  515.5 2.0 gather_fusion
  517.6 1.0 fusion.14
  518.6 0.0 reduce-scatter.11.cloned.1.call-start
  518.7 71.9 %reduce-scatter.9.cloned.1.call-done = f32[8,128]{1,0:T(8,128)} async-done(((f32[8,4096]{1,0:T(8,128)}), f32[8,128]{1,0:T(8,128)}) %reduce-scatter.9.cloned.1.call-update) | async-done | bytes 4112 | tf_op jit(solution)/shard_map/reduce_scatter | solution.py:91
  590.5 1.6 fusion.17
  592.1 0.0 reduce-scatter.13.cloned.1.call-start
  592.2 73.8 %reduce-scatter.11.cloned.1.call-done = f32[8,128]{1,0:T(8,128)} async-done(((f32[8,4096]{1,0:T(8,128)}), f32[8,128]{1,0:T(8,128)}) %reduce-scatter.11.cloned.1.call-update) | async-done | bytes 4112 | tf_op jit(solution)/shard_map/reduce_scatter | solution.py:94
  666.0 0.7 convert_element_type.38
  666.7 23.5 %all_gather.23 = bf16[8,4096]{1,0:T(8,128)(2,1)S(1)} all-gather(bf16[8,128]{1,0:T(8,128)(2,1)S(1)} %convert_element_type.38), channel_id=1, replica_groups=mesh['leaf'=4,'rows'=32] {'rows'}, dimensions={1}, use_global_device_ids=true | all-gather | bytes 67584 | tf_op jit(solution)/shard_map/all_gather | solution.py:95
  690.2 1.0 copy.72
  691.2 3.2 gather_fusion.1
  694.4 0.1 copy.73
  694.5 2.8 convolution_bitcast_fusion.1
  697.4 3.1 copy.76
  700.5 4.5 reshape.143
  705.0 0.0 reduce-scatter.15.cloned.1.call-start
  705.1 76.7 %reduce-scatter.13.cloned.1.call-done = f32[64,32]{1,0:T(8,128)} async-done(((f32[2048,32]{1,0:T(8,128)}), f32[64,32]{1,0:T(8,128)}) %reduce-scatter.13.cloned.1.call-update) | async-done | bytes 8208
  781.8 0.9 reshape.144
  782.7 0.1 copy.77
  782.8 0.3 convolution_bitcast_fusion
  783.0 3.1 copy.78
  786.1 4.5 reshape.145
  790.7 1.3 constant_dynamic-slice_fusion
  792.0 76.0 %reduce-scatter.15.cloned.1.call-done = f32[64,32]{1,0:T(8,128)} async-done(((f32[2048,32]{1,0:T(8,128)}), f32[64,32]{1,0:T(8,128)}) %reduce-scatter.15.cloned.1.call-update) | async-done | bytes 8208
  868.1 0.9 reshape.146
  868.9 0.7 copy.74
  (35 shorter events, 0.2 us)
Async XLA Ops:
  7.2 29.2 %copy-start = (bf16[4,64,2048]{2,1,0:T(8,128)(2,1)S(1)}, bf16[4,64,2048]{2,1,0:T(8,128)(2,1)}, u32[]{:S(2)}) copy-start(bf16[4,64,2048]{2,1,0:T(8,128)(2,1)} %param.15) | copy-start | bytes 3145732
  7.2 172.5 %all-reduce.5.cloned.1.call-start = ((), (), s32[]{:S(2)}) async-start(), calls=%async_computation.4 | async-start | bytes 524288 | tf_op jit(solution)/shard_map/psum | solution.py:54
  36.3 26.3 %copy-start.8 = (s32[4]{0:T(128)S(1)}, s32[4]{0:T(128)}, u32[]{:S(2)}) copy-start(s32[4]{0:T(128)} %param.18) | copy-start | bytes 52
  74.5 3.7 copy-start.9
  74.5 106.1 %copy-start.6 = (f32[8,1,128]{2,1,0:T(1,128)S(1)}, f32[8,1,128]{2,1,0:T(1,128)}, u32[]{:S(2)}) copy-start(f32[8,1,128]{2,1,0:T(1,128)} %param.13) | copy-start | bytes 12292
  74.5 130.7 %copy-start.3 = (bf16[1,128,4096]{2,1,0:T(8,128)(2,1)S(1)}, bf16[1,128,4096]{2,1,0:T(8,128)(2,1)}, u32[]{:S(2)}) copy-start(bf16[1,128,4096]{2,1,0:T(8,128)(2,1)} %param.19) | copy-start | bytes 3145732
  74.5 152.6 %copy-start.1 = (bf16[1,128,4096]{2,1,0:T(8,128)(2,1)S(1)}, bf16[1,128,4096]{2,1,0:T(8,128)(2,1)}, u32[]{:S(2)}) copy-start(bf16[1,128,4096]{2,1,0:T(8,128)(2,1)} %param.20) | copy-start | bytes 3145732
  78.1 253.0 %all-reduce.7.cloned.1.call-start = ((), (), s32[]{:S(2)}) async-start(), calls=%async_computation.5 | async-start | bytes 262144 | tf_op jit(solution)/shard_map/psum | solution.py:75
  227.6 103.5 %copy-start.5 = (f32[8,8192]{1,0:T(8,128)S(1)}, f32[8,8192]{1,0:T(8,128)}, u32[]{:S(2)}) copy-start(f32[8,8192]{1,0:T(8,128)} %all-reduce.5.cloned.1.call-done) | copy-start | bytes 786436
  227.6 146.8 %copy-start.7 = (f32[8,32]{1,0:T(8,128)S(1)}, f32[8,32]{1,0:T(8,128)}, u32[]{:S(2)}) copy-start(f32[8,32]{1,0:T(8,128)} %param.14) | copy-start | bytes 3076
  230.4 144.0 %all-reduce.11.cloned.1.call-start = ((), (), s32[]{:S(2)}) async-start(), calls=%async_computation.9 | async-start | bytes 262144 | tf_op jit(solution)/shard_map/psum | solution.py:56
  332.8 180.6 %all-reduce.9.cloned.1.call-start = ((), (), s32[]{:S(2)}) async-start(), calls=%async_computation.6 | async-start | bytes 262144 | tf_op jit(solution)/shard_map/psum | solution.py:85
  411.1 106.5 %copy-start.2 = (bf16[1,128,4096]{2,1,0:T(8,128)(2,1)S(1)}, bf16[1,128,4096]{2,1,0:T(8,128)(2,1)}, u32[]{:S(2)}) copy-start(bf16[1,128,4096]{2,1,0:T(8,128)(2,1)} %param.20) | copy-start | bytes 3145732
  411.4 179.2 %copy-start.4 = (bf16[1,128,4096]{2,1,0:T(8,128)(2,1)S(1)}, bf16[1,128,4096]{2,1,0:T(8,128)(2,1)}, u32[]{:S(2)}) copy-start(bf16[1,128,4096]{2,1,0:T(8,128)(2,1)} %param.19) | copy-start | bytes 3145732
  414.6 176.0 %reduce-scatter.9.cloned.1.call-start = ((), (), s32[]{:S(2)}) async-start(), calls=%async_computation.7 | async-start | bytes 135168 | tf_op jit(solution)/shard_map/reduce_scatter | solution.py:91
  518.6 147.3 %reduce-scatter.11.cloned.1.call-start = ((), (), s32[]{:S(2)}) async-start(), calls=%async_computation.8 | async-start | bytes 135168 | tf_op jit(solution)/shard_map/reduce_scatter | solution.py:94
  592.1 189.7 %reduce-scatter.13.cloned.1.call-start = ((), (), s32[]{:S(2)}) async-start(), calls=%async_computation.10 | async-start | bytes 1081344
  705.0 163.0 %reduce-scatter.15.cloned.1.call-start = ((), (), s32[]{:S(2)}) async-start(), calls=%async_computation.11 | async-start | bytes 1081344
Sparse Core Ops, SparseCore 0:
  78.3 101.3 all-reduce.4
  230.5 100.5 all-reduce.6
  333.5 40.8 all-reduce.10
  414.7 98.5 all-reduce.8
  518.7 71.7 reduce-scatter.8
  594.4 71.5 reduce-scatter.10
  705.2 76.6 reduce-scatter.12
  790.8 77.2 reduce-scatter.14
